TPU v7x, 256 devices: a whole 4x4x8 slice. The times are simulated.
256 devices in a mesh: leaf: 16 (over y, x), row: 16 (over z, core).
Axes of the slice: x: 4, y: 4, z: 8, core: 2. Of those that a mesh axis runs over, the one named last changes fastest.
Arguments:
- sigma_root: float32 [2048, 2048], P(None, 'row')
- linv_one: bfloat16 [16, 2048, 2048], P('leaf', None, 'row'), as said below
- panel_one: bfloat16 [16, 512, 2048], P('leaf', None, 'row'), may hold values from -1.25 to 1.25
- tiles_one: int32 [16, 4], replicated, may hold values from 0 to 15, as said below
- mask_one: int32 [16, 4, 16], P('leaf', None, 'row'), may hold values 0 or 1
- linv_two: bfloat16 [16, 2048, 2048], P('leaf', None, 'row'), as said below
- panel_two: bfloat16 [16, 512, 2048], P('leaf', None, 'row'), may hold values from -1.25 to 1.25
- tiles_two: int32 [16, 4], replicated, may hold values from 0 to 15, as said below
- mask_two: int32 [16, 4, 16], P('leaf', None, 'row'), may hold values 0 or 1
- parent: int32 [16], replicated, may hold values from 0 to 15
Outputs:
- sigma_one: float32 [16, 2048, 2048], P('leaf', None, 'row')
- cross_one: float32 [16, 512, 2048], P('leaf', None, 'row')
- sigma_two: float32 [16, 2048, 2048], P('leaf', None, 'row')
- cross_two: float32 [16, 512, 2048], P('leaf', None, 'row')
Inputs may be any that keep to these rules, and one draw needn't show every extreme that they name: `tiles_one`: each row holds 4 different tile numbers in increasing order. `tiles_two`: each row holds 4 different tile numbers in increasing order. `linv_one`: each block is lower triangular with a positive diagonal. `sigma_root`: symmetric. `linv_two`: each block is lower triangular with a positive diagonal.
All inputs are finite; a program needn't handle non-finite values. No bound on the sum of `mask_one` or of `mask_two` on one device may be relied on, other than what follows from the above.
Results may differ from a plain program's by a relative error of at most 0.00045.
Values may be sent and summed in bfloat16 or wider, within the bound.
No kernel may reach another device: no remote copies, remote signals or barrier semaphores. Data moves between devices by JAX's collectives and lax.ppermute only.
A program may use at most 64 MiB of HBM per device.

v0:
```python
import jax
import jax.numpy as jnp
from jax import lax
from jax.sharding import PartitionSpec as P

TILE = 128


def pattern_rows(tile_list):
    offsets = jnp.arange(TILE, dtype=jnp.int32)
    return (tile_list[..., None] * TILE + offsets).reshape(tile_list.shape[:-1] + (-1,))


def expand_mask(tile_mask):
    return jnp.repeat(jnp.repeat(tile_mask, TILE, axis=0), TILE, axis=1)


def assemble(selected, row_list):
    gathered = lax.all_gather(selected, "row", axis=1, tiled=True)
    return jnp.take(gathered, row_list, axis=1)


def solve_block(selected, row_list, linv_local, panel_local, mask_local):
    select = assemble(selected, row_list)
    masked = panel_local * expand_mask(mask_local).astype(jnp.bfloat16)
    linv_wide = linv_local.astype(jnp.float32)
    whole_panel = lax.all_gather(masked, "row", axis=1, tiled=True)
    upper_part = jnp.dot(whole_panel, linv_local, preferred_element_type=jnp.float32)
    cross = -jnp.dot(select, upper_part, precision=lax.Precision.HIGHEST)
    middle = linv_wide - jnp.dot(
        whole_panel.astype(jnp.float32).T, cross, precision=lax.Precision.HIGHEST
    )
    sigma = jnp.dot(
        lax.all_gather(linv_local, "row", axis=1, tiled=True).astype(jnp.float32).T,
        middle,
        precision=lax.Precision.HIGHEST,
    )
    return (sigma, cross)


def body(
    sigma_root,
    linv_one,
    panel_one,
    tiles_one,
    mask_one,
    linv_two,
    panel_two,
    tiles_two,
    mask_two,
    parent,
):
    leaf_id = lax.axis_index("leaf")
    width = sigma_root.shape[1]
    own_tiles = lax.dynamic_index_in_dim(tiles_one, leaf_id, 0, keepdims=False)
    rows_first = pattern_rows(own_tiles)
    selected_first = jnp.take(sigma_root, rows_first, axis=0)
    sigma_first, cross_first = solve_block(
        selected_first, rows_first, linv_one[0], panel_one[0], mask_one[0]
    )
    rows_every = pattern_rows(tiles_two)
    count = rows_every.shape[0]
    block_rows = rows_every.shape[1]
    owned = (parent == leaf_id).astype(jnp.float32)
    slots = jnp.take(sigma_first, rows_every.reshape(-1), axis=0).reshape(count, block_rows, width)
    slots = slots * owned[:, None, None]
    arrived = lax.all_to_all(slots, "leaf", split_axis=0, concat_axis=0, tiled=True)
    selected_second = jnp.sum(arrived, axis=0)
    rows_second = lax.dynamic_index_in_dim(rows_every, leaf_id, 0, keepdims=False)
    sigma_second, cross_second = solve_block(
        selected_second, rows_second, linv_two[0], panel_two[0], mask_two[0]
    )
    return (sigma_first[None], cross_first[None], sigma_second[None], cross_second[None])


def solution(mesh):
    return jax.shard_map(
        body,
        mesh=mesh,
        in_specs=(
            P(None, "row"),
            P("leaf", None, "row"),
            P("leaf", None, "row"),
            P(),
            P("leaf", None, "row"),
            P("leaf", None, "row"),
            P("leaf", None, "row"),
            P(),
            P("leaf", None, "row"),
            P(),
        ),
        out_specs=(
            P("leaf", None, "row"),
            P("leaf", None, "row"),
            P("leaf", None, "row"),
            P("leaf", None, "row"),
        ),
        check_vma=False,
    )
```

profile of v0, /device:TPU:1, one launch (start us, length us, event | category | flops | bytes accessed | tf_op | source)
XLA Modules:
  0.0 404.3 jit_solution(16791441184361963141)
XLA Ops:
  8.1 1.7 bitcast_multiply_fusion.1
  16.1 39.5 %all-gather.9.cloned.1.call-done = bf16[512,2048]{1,0:T(8,128)(2,1)} async-done(((bf16[512,128]{1,0:T(8,128)(2,1)}), bf16[512,2048]{1,0:T(8,128)(2,1)}) %all-gather.9.cloned.1.call-update) | async-done | bytes 2097168 | tf_op jit(solution)/shard_map/all_gather | solution.py:27
  55.5 2.3 fusion.13
  57.8 48.6 %all-gather.11.cloned.1.call-done = f32[512,2048]{1,0:T(8,128)} async-done(((f32[512,128]{1,0:T(8,128)}), f32[512,2048]{1,0:T(8,128)}) %all-gather.11.cloned.1.call-update) | async-done | bytes 4194320 | tf_op jit(solution)/shard_map/all_gather | solution.py:19
  106.5 5.3 %copy.19 = f32[512,2048]{0,1:T(8,128)} copy(f32[512,2048]{1,0:T(8,128)} %all-gather.11.cloned.1.call-done) | data formatting | bytes 8388608 | tf_op jit(solution)/shard_map/all_gather | solution.py:19
  111.8 4.2 %gather_fusion.2 = f32[512,512]{1,0:T(8,128)S(1)} fusion(f32[512,2048]{0,1:T(8,128)} %copy.19, s32[1024]{0:T(1024)S(1)} %pad_clamp_fusion.1), kind=kCustom, calls=%fused_computation.clone | custom fusion | bytes 2099200 | tf_op jit(solution)/shard_map/jit(_take)/gather | solution.py:20
  116.0 1.9 convolution_negate_fusion.1
  118.6 3.9 convolution_subtract_fusion.1
  122.6 50.3 %all-gather.17.cloned.1.call-done = bf16[1,2048,2048]{2,1,0:T(8,128)(2,1)} async-done(((bf16[1,2048,128]{2,1,0:T(8,128)(2,1)}), bf16[1,2048,2048]{2,1,0:T(8,128)(2,1)}) %all-gather.17.cloned.1.call-update) | async-done | bytes 8388624 | tf_op jit(solution)/shard_map/all_gather | solution.py:34
  172.9 6.3 %fusion.2 = f32[128,2048]{1,0:T(8,128)S(1)} fusion(f32[2048,128]{1,0:T(8,128)S(1)} %convolution_subtract_fusion.1, bf16[1,2048,2048]{2,1,0:T(8,128)(2,1)} %all-gather.17.cloned.1.call-done), kind=kOutput, calls=%fused_computation.6 | convolution fusion | flops 6442450944 | bytes 10485760 | tf_op jit(solution)/shard_map/dot_general | solution.py:33
  179.5 27.8 %gather_fusion.1 = f32[8192,128]{1,0:T(8,128)} fusion(f32[2048,128]{1,0:T(8,128)S(1)} %copy.21, s32[8192]{0:T(1024)S(1)} %broadcast_clamp_fusion), kind=kCustom, calls=%fused_computation.3 | custom fusion | bytes 8421376 | tf_op jit(solution)/shard_map/jit(_take)/gather | solution.py:65
  207.3 5.3 %select_multiply_fusion = f32[16,512,128]{2,1,0:T(8,128)} fusion(f32[16,512,128]{2,1,0:T(8,128)} %bitcast.84, f32[16]{0:T(128)S(1)} %compare_convert_fusion, pred[16,512]{1,0:T(8,128)(4,1)S(1)} %compare_and_fusion), kind=kLoop, calls=%fused_computation.8 | loop fusion | flops 2097152 | bytes 8396864 | tf_op jit(solution)/shard_map/mul | solution.py:66
  212.5 4.7 %all-to-all-start = ((f32[16,512,128]{2,1,0:T(8,128)}), f32[16,512,128]{2,1,0:T(8,128)}, u32[]{:S(2)}, u32[]{:S(2)}) async-start(f32[16,512,128]{2,1,0:T(8,128)} %select_multiply_fusion), calls=%async_computation | async-start | bytes 8388608 | tf_op jit(solution)/shard_map/all_to_all | solution.py:67
  218.2 62.3 %all-to-all-done = f32[16,512,128]{2,1,0:T(8,128)} async-done(((f32[16,512,128]{2,1,0:T(8,128)}), f32[16,512,128]{2,1,0:T(8,128)}, u32[]{:S(2)}, u32[]{:S(2)}) %all-to-all-start) | async-done | bytes 4194336 | tf_op jit(solution)/shard_map/all_to_all | solution.py:67
  280.5 2.4 reduce_sum.9
  284.4 2.3 fusion.11
  286.7 1.3 copy.23
  288.0 35.5 %all-gather.15.cloned.1.call-done = f32[512,2048]{0,1:T(8,128)} async-done(((f32[512,128]{0,1:T(8,128)}), f32[512,2048]{0,1:T(8,128)}) %all-gather.15.cloned.1.call-update) | async-done | bytes 4194320 | tf_op jit(solution)/shard_map/all_gather | solution.py:19
  323.6 4.2 %gather_fusion.3 = f32[512,512]{1,0:T(8,128)S(1)} fusion(f32[512,2048]{0,1:T(8,128)} %all-gather.15.cloned.1.call-done, s32[1024]{0:T(1024)S(1)} %pad_clamp_fusion), kind=kCustom, calls=%fused_computation.1.clone | custom fusion | bytes 2099200 | tf_op jit(solution)/shard_map/jit(_take)/gather | solution.py:20
  327.8 1.9 convolution_negate_fusion
  329.7 4.0 convolution_subtract_fusion
  333.7 56.2 %all-gather.19.cloned.1.call-done = bf16[1,2048,2048]{2,1,0:T(8,128)(2,1)} async-done(((bf16[1,2048,128]{2,1,0:T(8,128)(2,1)}), bf16[1,2048,2048]{2,1,0:T(8,128)(2,1)}) %all-gather.19.cloned.1.call-update) | async-done | bytes 8388624 | tf_op jit(solution)/shard_map/all_gather | solution.py:34
  389.9 6.3 %fusion.4 = f32[1,2048,128]{1,2,0:T(8,128)S(1)} fusion(f32[2048,128]{1,0:T(8,128)S(1)} %convolution_subtract_fusion, bf16[1,2048,2048]{2,1,0:T(8,128)(2,1)} %all-gather.19.cloned.1.call-done), kind=kOutput, calls=%fused_computation.9 | convolution fusion | flops 6442450944 | bytes 10485760 | tf_op jit(solution)/shard_map/dot_general | solution.py:33
  396.2 1.3 copy.24
  (58 shorter events, 10.5 us)
Async XLA Ops:
  7.2 3.6 copy-start
  7.2 48.4 %copy-start.1 = (bf16[1,2048,128]{2,1,0:T(8,128)(2,1)S(1)}, bf16[1,2048,128]{2,1,0:T(8,128)(2,1)}, u32[]{:S(2)}) copy-start(bf16[1,2048,128]{2,1,0:T(8,128)(2,1)} %param.13) | copy-start | bytes 1572868
  7.2 48.3 %all-gather.9.cloned.1.call-start = ((), (), s32[]{:S(2)}) async-start(), calls=%async_computation.1 | async-start | bytes 2228224 | tf_op jit(solution)/shard_map/all_gather | solution.py:27
  9.8 96.7 %all-gather.11.cloned.1.call-start = ((), (), s32[]{:S(2)}) async-start(), calls=%async_computation.2 | async-start | bytes 4456448 | tf_op jit(solution)/shard_map/all_gather | solution.py:19
  12.8 160.1 %all-gather.17.cloned.1.call-start = ((), (), s32[]{:S(2)}) async-start(), calls=%async_computation.5 | async-start | bytes 8912896 | tf_op jit(solution)/shard_map/all_gather | solution.py:34
  117.9 0.7 copy-start.4
  212.5 4.8 %copy-start.6 = (bf16[1,512,128]{2,1,0:T(8,128)(2,1)S(1)}, bf16[1,512,128]{2,1,0:T(8,128)(2,1)}, u32[]{:S(2)}) copy-start(bf16[1,512,128]{2,1,0:T(8,128)(2,1)} %param.18) | copy-start | bytes 393220
  212.5 67.9 %all-to-all-start = ((f32[16,512,128]{2,1,0:T(8,128)}), f32[16,512,128]{2,1,0:T(8,128)}, u32[]{:S(2)}, u32[]{:S(2)}) async-start(f32[16,512,128]{2,1,0:T(8,128)} %select_multiply_fusion), calls=%async_computation | async-start | bytes 8388608 | tf_op jit(solution)/shard_map/all_to_all | solution.py:67
  217.2 67.2 %copy-start.2 = (bf16[1,2048,128]{2,1,0:T(8,128)(2,1)S(1)}, bf16[1,2048,128]{2,1,0:T(8,128)(2,1)}, u32[]{:S(2)}) copy-start(bf16[1,2048,128]{2,1,0:T(8,128)(2,1)} %param.17) | copy-start | bytes 1572868
  217.2 67.2 %all-gather.13.cloned.1.call-start = ((), (), s32[]{:S(2)}) async-start(), calls=%async_computation.3 | async-start | bytes 2228224 | tf_op jit(solution)/shard_map/all_gather | solution.py:27
  218.1 105.4 %all-gather.15.cloned.1.call-start = ((), (), s32[]{:S(2)}) async-start(), calls=%async_computation.4 | async-start | bytes 4456448 | tf_op jit(solution)/shard_map/all_gather | solution.py:19
  283.7 106.2 %all-gather.19.cloned.1.call-start = ((), (), s32[]{:S(2)}) async-start(), calls=%async_computation.6 | async-start | bytes 8912896 | tf_op jit(solution)/shard_map/all_gather | solution.py:34
  288.0 41.6 %copy-start.3 = (bf16[1,2048,128]{2,1,0:T(8,128)(2,1)S(1)}, bf16[1,2048,128]{2,1,0:T(8,128)(2,1)}, u32[]{:S(2)}) copy-start(bf16[1,2048,128]{2,1,0:T(8,128)(2,1)} %param.17) | copy-start | bytes 1572868
  329.7 4.0 copy-start.5
Sparse Core Ops, SparseCore 0:
  10.4 45.1 all-gather.8
  57.9 48.5 all-gather.10
  108.2 64.6 all-gather.16
  220.1 40.0 all-gather.12
  283.9 39.6 all-gather.14
  325.2 64.6 all-gather.18
where the time goes:
time: 405 us; the launch traced here: 404 us
  waiting for transfers between devices  294 us (73%)
  local copies, waits for them, and re-layouts  47.4 us (12%)
  matrix products  28.8 us (7%)
  other arithmetic  15.1 us (4%)
  between operations  14.4 us (4%)
  starting transfers between devices  5.12 us (1%)
    all_gather x2, waiting for transfers between devices, solve_block(): lax.all_gather(linv_local, 'row', axis=1, tiled=True).astype(jnp.float32)  107 us
    all_gather x2, waiting for transfers between devices, assemble(): gathered = lax.all_gather(selected, 'row', axis=1, tiled=True)  84.1 us
    all_to_all x1, waiting for transfers between devices, body(): lax.all_to_all(slots, 'leaf', split_axis=0, concat_axis=0, tiled=True)  62.3 us
    all_gather x2, waiting for transfers between devices, solve_block(): whole_panel = lax.all_gather(masked, 'row', axis=1, tiled=True)  39.5 us
    gather x1, local copies, waits for them, and re-layouts, body(): jnp.take(sigma_first, rows_every.reshape(-1), axis=0)  27.8 us
    dot_general x2, matrix products, solve_block(): jnp.dot(lax.all_gather(linv_local, 'row', axis=1, tiled=True).astype(jnp....  12.5 us
    gather x2, local copies, waits for them, and re-layouts, assemble(): return jnp.take(gathered, row_list, axis=1)  8.43 us
  transfers between devices with their start and end apart: 7, of which 6 were waited for; matrix products, arithmetic and copies ran while one was open for 10% of the time, Pallas kernels for 0%

commit v1 on v0

--- a/solution.py
+++ b/solution.py
@@ -4,6 +4,11 @@
 from jax.sharding import PartitionSpec as P
 
 TILE = 128
+
+
+def gather_from_all(x, axis, dim):
+    copies = jnp.concatenate([x] * lax.axis_size(axis), axis=dim)
+    return lax.all_to_all(copies, axis, dim, dim, tiled=True)
 
 
 def pattern_rows(tile_list):
@@ -24,7 +29,7 @@
     select = assemble(selected, row_list)
     masked = panel_local * expand_mask(mask_local).astype(jnp.bfloat16)
     linv_wide = linv_local.astype(jnp.float32)
-    whole_panel = lax.all_gather(masked, "row", axis=1, tiled=True)
+    whole_panel = gather_from_all(masked, "row", 1)
     upper_part = jnp.dot(whole_panel, linv_local, preferred_element_type=jnp.float32)
     cross = -jnp.dot(select, upper_part, precision=lax.Precision.HIGHEST)
     middle = linv_wide - jnp.dot(

time: 405 us -> 422 us (1.042)
  blocking collectives: 0 us -> 54.4 us
  waiting for transfers between devices: 294 us -> 242 us
  starting transfers between devices: 5.12 us -> 16.4 us
  local copies, waits for them, and re-layouts: 47.4 us -> 57.5 us
  other arithmetic: 15.1 us -> 10.1 us
    all_gather x2, waiting for transfers between devices: 84.1 us -> 12.5 us  [assemble(): gathered = lax.all_gather(selected, 'row', axis=1, tiled=True)]
    all_to_all x1 -> x2, waiting for transfers between devices: 62.3 us -> 125 us  [gather_from_all(): return lax.all_to_all(copies, axis, dim, dim, tiled=True)]
    all_to_all x0 -> x1, blocking collectives: none -> 54.4 us  [body(): lax.all_to_all(slots, 'leaf', split_axis=0, concat_axis=0, tiled=True)]
    all_gather x2 -> x0, waiting for transfers between devices: 39.5 us -> none  [solve_block(): whole_panel = lax.all_gather(masked, 'row', axis=1, tiled=True)]
    all_to_all x1 -> x2, starting transfers between devices: 4.69 us -> 16.3 us  [gather_from_all(): return lax.all_to_all(copies, axis, dim, dim, tiled=True)]
    all_to_all x0 -> x2, local copies, waits for them, and re-layouts: none -> 5.73 us  [gather_from_all(): return lax.all_to_all(copies, axis, dim, dim, tiled=True)]
  transfers between devices with their start and end apart: 7 -> 6, of which waited for: 6 -> 5; matrix products, arithmetic and copies ran while one was open for 10% -> 10% of each run, Pallas kernels for 0% -> 0%
where the time goes in v1:
time: 422 us; the launch traced here: 421 us
  waiting for transfers between devices  242 us (57%)
  local copies, waits for them, and re-layouts  57.5 us (14%)
  blocking collectives  54.4 us (13%)
  matrix products  26.1 us (6%)
  starting transfers between devices  16.4 us (4%)
  between operations  14.1 us (3%)
  other arithmetic  10.1 us (2%)
    all_to_all x2, waiting for transfers between devices, gather_from_all(): return lax.all_to_all(copies, axis, dim, dim, tiled=True)  125 us
    all_gather x2, waiting for transfers between devices, solve_block(): lax.all_gather(linv_local, 'row', axis=1, tiled=True).astype(jnp.float32)  104 us
    all_to_all x1, blocking collectives, body(): lax.all_to_all(slots, 'leaf', split_axis=0, concat_axis=0, tiled=True)  54.4 us
    gather x1, local copies, waits for them, and re-layouts, body(): jnp.take(sigma_first, rows_every.reshape(-1), axis=0)  27.9 us
    all_to_all x2, starting transfers between devices, gather_from_all(): return lax.all_to_all(copies, axis, dim, dim, tiled=True)  16.3 us
    dot_general x2, matrix products, solve_block(): jnp.dot(lax.all_gather(linv_local, 'row', axis=1, tiled=True).astype(jnp....  12.9 us
    all_gather x2, waiting for transfers between devices, assemble(): gathered = lax.all_gather(selected, 'row', axis=1, tiled=True)  12.5 us
    gather x2, local copies, waits for them, and re-layouts, assemble(): return jnp.take(gathered, row_list, axis=1)  9.18 us
  transfers between devices with their start and end apart: 6, of which 5 were waited for; matrix products, arithmetic and copies ran while one was open for 10% of the time, Pallas kernels for 0%

profile of v1, /device:TPU:1, one launch (start us, length us, event | category | flops | bytes accessed | tf_op | source)
XLA Modules:
  0.0 421.0 jit_solution(16666683376809430414)
XLA Ops:
  12.9 1.7 concatenate.8
  14.6 10.1 %all-to-all-start = ((bf16[512,16,128]{2,0,1:T(8,128)(2,1)}), bf16[512,16,128]{2,0,1:T(8,128)(2,1)}, u32[]{:S(2)}, u32[]{:S(2)}) async-start(bf16[512,16,128]{2,0,1:T(8,128)(2,1)} %concatenate.8), calls=%async_computation | async-start | bytes 4194304 | tf_op jit(solution)/shard_map/all_to_all | solution.py:11
  25.2 59.7 %all-to-all-done = bf16[512,16,128]{2,0,1:T(8,128)(2,1)} async-done(((bf16[512,16,128]{2,0,1:T(8,128)(2,1)}), bf16[512,16,128]{2,0,1:T(8,128)(2,1)}, u32[]{:S(2)}, u32[]{:S(2)}) %all-to-all-start) | async-done | bytes 2097184 | tf_op jit(solution)/shard_map/all_to_all | solution.py:11
  84.9 2.9 copy.25
  88.5 12.5 %all-gather.7.cloned.1.call-done = f32[512,2048]{1,0:T(8,128)} async-done(((f32[512,128]{1,0:T(8,128)}), f32[512,2048]{1,0:T(8,128)}) %all-gather.7.cloned.1.call-update) | async-done | bytes 4194320 | tf_op jit(solution)/shard_map/all_gather | solution.py:24
  101.0 5.3 %copy.26 = f32[512,2048]{0,1:T(8,128)} copy(f32[512,2048]{1,0:T(8,128)} %all-gather.7.cloned.1.call-done) | data formatting | bytes 8388608 | tf_op jit(solution)/shard_map/all_gather | solution.py:24
  106.3 4.2 %gather_fusion.2 = f32[512,512]{1,0:T(8,128)S(1)} fusion(f32[512,2048]{0,1:T(8,128)} %copy.26, s32[1024]{0:T(1024)S(1)} %pad_clamp_fusion.1), kind=kCustom, calls=%fused_computation.clone | custom fusion | bytes 2099200 | tf_op jit(solution)/shard_map/jit(_take)/gather | solution.py:25
  110.6 1.9 convolution_negate_fusion.1
  113.2 2.9 convolution_subtract_fusion.1
  116.0 51.9 %all-gather.11.cloned.1.call-done = bf16[1,2048,2048]{2,1,0:T(8,128)(2,1)} async-done(((bf16[1,2048,128]{2,1,0:T(8,128)(2,1)}), bf16[1,2048,2048]{2,1,0:T(8,128)(2,1)}) %all-gather.11.cloned.1.call-update) | async-done | bytes 8388624 | tf_op jit(solution)/shard_map/all_gather | solution.py:39
  167.9 6.3 %fusion.2 = f32[128,2048]{1,0:T(8,128)S(1)} fusion(f32[2048,128]{1,0:T(8,128)S(1)} %convolution_subtract_fusion.1, bf16[1,2048,2048]{2,1,0:T(8,128)(2,1)} %all-gather.11.cloned.1.call-done), kind=kOutput, calls=%fused_computation.6 | convolution fusion | flops 6442450944 | bytes 10485760 | tf_op jit(solution)/shard_map/dot_general | solution.py:38
  174.5 27.9 %gather_fusion.1 = f32[8192,128]{1,0:T(8,128)} fusion(f32[2048,128]{1,0:T(8,128)S(1)} %copy.29, s32[8192]{0:T(1024)S(1)} %broadcast_clamp_fusion), kind=kCustom, calls=%fused_computation.3 | custom fusion | bytes 8421376 | tf_op jit(solution)/shard_map/jit(_take)/gather | solution.py:70
  202.4 3.6 select_multiply_fusion
  206.0 54.4 %all_to_all.23 = f32[16,512,128]{2,1,0:T(8,128)} all-to-all(f32[16,512,128]{2,1,0:T(8,128)S(1)} %select_multiply_fusion), channel_id=1, replica_groups=mesh['leaf'=16,'row'=16] {'leaf'}, dimensions={0} | all-to-all | bytes 8388608 | tf_op jit(solution)/shard_map/all_to_all | solution.py:72
  260.4 2.5 reduce_sum.9
  266.2 6.2 %all-to-all-start.1 = ((bf16[512,16,128]{2,0,1:T(8,128)(2,1)}), bf16[512,16,128]{2,0,1:T(8,128)(2,1)}, u32[]{:S(2)}, u32[]{:S(2)}) async-start(bf16[512,16,128]{2,0,1:T(8,128)(2,1)} %concatenate.9), calls=%async_computation.1 | async-start | bytes 4194304 | tf_op jit(solution)/shard_map/all_to_all | solution.py:11
  272.5 65.5 %all-to-all-done.1 = bf16[512,16,128]{2,0,1:T(8,128)(2,1)} async-done(((bf16[512,16,128]{2,0,1:T(8,128)(2,1)}), bf16[512,16,128]{2,0,1:T(8,128)(2,1)}, u32[]{:S(2)}, u32[]{:S(2)}) %all-to-all-start.1) | async-done | bytes 2097184 | tf_op jit(solution)/shard_map/all_to_all | solution.py:11
  338.0 2.9 copy.27
  340.8 1.8 fusion.11
  343.9 5.0 %gather_fusion.3 = f32[512,512]{1,0:T(8,128)} fusion(f32[512,2048]{0,1:T(8,128)} %all-gather.9.cloned.1.call-done, s32[1024]{0:T(1024)S(1)} %pad_clamp_fusion), kind=kCustom, calls=%fused_computation.1.clone | custom fusion | bytes 2099200 | tf_op jit(solution)/shard_map/jit(_take)/gather | solution.py:25
  348.9 3.1 convolution_negate_fusion
  352.0 2.8 convolution_subtract_fusion
  354.8 51.6 %all-gather.13.cloned.1.call-done = bf16[1,2048,2048]{2,1,0:T(8,128)(2,1)} async-done(((bf16[1,2048,128]{2,1,0:T(8,128)(2,1)}), bf16[1,2048,2048]{2,1,0:T(8,128)(2,1)}) %all-gather.13.cloned.1.call-update) | async-done | bytes 8388624 | tf_op jit(solution)/shard_map/all_gather | solution.py:39
  406.5 6.6 %fusion.4 = f32[1,2048,128]{1,2,0:T(8,128)S(1)} fusion(f32[2048,128]{1,0:T(8,128)} %convolution_subtract_fusion, bf16[1,2048,2048]{2,1,0:T(8,128)(2,1)} %all-gather.13.cloned.1.call-done), kind=kOutput, calls=%fused_computation.9 | convolution fusion | flops 6442450944 | bytes 10485760 | tf_op jit(solution)/shard_map/dot_general | solution.py:38
  (69 shorter events, 13.9 us)
Async XLA Ops:
  7.2 1.2 copy-start
  7.2 93.8 %all-gather.7.cloned.1.call-start = ((), (), s32[]{:S(2)}) async-start(), calls=%async_computation.3 | async-start | bytes 4456448 | tf_op jit(solution)/shard_map/all_gather | solution.py:24
  9.4 15.3 %copy-start.9 = (s32[16,4]{0,1:T(4,128)S(1)}, s32[16,4]{0,1:T(4,128)}, u32[]{:S(2)}) copy-start(s32[16,4]{0,1:T(4,128)} %param.19) | copy-start | bytes 772
  9.5 15.5 %copy-start.10 = (s32[16]{0:T(128)S(1)}, s32[16]{0:T(128)}, u32[]{:S(2)}) copy-start(s32[16]{0:T(128)} %param.21) | copy-start | bytes 196
  10.3 157.6 %all-gather.11.cloned.1.call-start = ((), (), s32[]{:S(2)}) async-start(), calls=%async_computation.5 | async-start | bytes 8912896 | tf_op jit(solution)/shard_map/all_gather | solution.py:39
  14.6 73.2 %copy-start.4 = (bf16[1,2048,128]{2,1,0:T(8,128)(2,1)S(1)}, bf16[1,2048,128]{2,1,0:T(8,128)(2,1)}, u32[]{:S(2)}) copy-start(bf16[1,2048,128]{2,1,0:T(8,128)(2,1)} %param.13) | copy-start | bytes 1572868
  14.6 70.3 %all-to-all-start = ((bf16[512,16,128]{2,0,1:T(8,128)(2,1)}), bf16[512,16,128]{2,0,1:T(8,128)(2,1)}, u32[]{:S(2)}, u32[]{:S(2)}) async-start(bf16[512,16,128]{2,0,1:T(8,128)(2,1)} %concatenate.8), calls=%async_computation | async-start | bytes 4194304 | tf_op jit(solution)/shard_map/all_to_all | solution.py:11
  24.7 319.2 %all-gather.9.cloned.1.call-start = ((), (), s32[]{:S(2)}) async-start(), calls=%async_computation.4 | async-start | bytes 4456448 | tf_op jit(solution)/shard_map/all_gather | solution.py:24
  112.5 0.7 copy-start.6
  174.2 28.2 %copy-start.2 = (f32[128,2048]{1,0:T(8,128)}, f32[128,2048]{1,0:T(8,128)S(1)}, u32[]{:S(2)}) copy-start(f32[128,2048]{1,0:T(8,128)S(1)} %fusion.2) | copy-start | bytes 3145732
  260.4 3.9 copy-start.11
  260.4 4.0 copy-start.8
  263.7 142.8 %all-gather.13.cloned.1.call-start = ((), (), s32[]{:S(2)}) async-start(), calls=%async_computation.6 | async-start | bytes 8912896 | tf_op jit(solution)/shard_map/all_gather | solution.py:39
  266.2 71.7 %all-to-all-start.1 = ((bf16[512,16,128]{2,0,1:T(8,128)(2,1)}), bf16[512,16,128]{2,0,1:T(8,128)(2,1)}, u32[]{:S(2)}, u32[]{:S(2)}) async-start(bf16[512,16,128]{2,0,1:T(8,128)(2,1)} %concatenate.9), calls=%async_computation.1 | async-start | bytes 4194304 | tf_op jit(solution)/shard_map/all_to_all | solution.py:11
  272.4 70.2 %copy-start.3 = (f32[128,2048]{1,0:T(8,128)S(1)}, f32[128,2048]{1,0:T(8,128)}, u32[]{:S(2)}) copy-start(f32[128,2048]{1,0:T(8,128)} %copy-done.2) | copy-start | bytes 3145732
  343.9 8.1 %copy-start.5 = (bf16[1,2048,128]{2,1,0:T(8,128)(2,1)S(1)}, bf16[1,2048,128]{2,1,0:T(8,128)(2,1)}, u32[]{:S(2)}) copy-start(bf16[1,2048,128]{2,1,0:T(8,128)(2,1)} %param.17) | copy-start | bytes 1572868
  352.0 2.8 copy-start.7
  406.5 8.0 %copy-start.1 = (f32[2048,128]{1,0:T(8,128)S(1)}, f32[2048,128]{1,0:T(8,128)}, u32[]{:S(2)}) copy-start(f32[2048,128]{1,0:T(8,128)} %param.12) | copy-start | bytes 3145732
Sparse Core Ops, SparseCore 0:
  10.5 90.5 all-gather.6
  102.8 65.1 all-gather.10
  263.8 77.4 all-gather.8
  343.0 63.4 all-gather.12
